TPU v7x, 512 devices: a whole 4x8x8 slice. The times are simulated.
512 devices in a mesh: pair: 64 (over z, x, core), slab: 8 (over y).
Axes of the slice: x: 4, y: 8, z: 8, core: 2. Of those that a mesh axis runs over, the one named last changes fastest.
Arguments:
- amps: bfloat16 [1024, 1024, 128], P(('pair', 'slab')), may hold values from -6 to 6
- symmetry: int32 [1024], replicated, may hold values from 0 to 3
- screen: int32 [64, 16, 16], P('pair'), may hold values 0 or 1
- owner: int32 [1024], replicated, may hold values from 0 to 63, as said below
- integrals: bfloat16 [64, 2048, 2048], P('pair', 'slab'), may hold values from -0.25 to 0.25
Outputs:
- residual: bfloat16 [1024, 64, 16, 128], P(('pair', 'slab'))
Inputs may be any that keep to these rules, and one draw needn't show every extreme that they name: Every owner from 0 to 63 holds exactly 16 tiles.
All inputs are finite; a program needn't handle non-finite values. No bound on the sum of `screen` on one device may be relied on, other than what follows from the above.
Results may differ from a plain program's by a relative error of at most 0.001.
Values may be sent and summed in bfloat16 or wider, within the bound.
A program may use at most 64 MiB of HBM per device.

v0:
```python
import jax
import jax.numpy as jnp
from jax import lax
from jax.sharding import PartitionSpec as P


def contract(operand, block_piece, mask_piece, per_owner, tile_width):
    rows_here = block_piece.shape[0]
    masked = (
        block_piece.reshape(rows_here, per_owner, tile_width) * mask_piece[:, :, None]
    ).reshape(rows_here, per_owner * tile_width)
    return jnp.dot(operand, masked, preferred_element_type=jnp.float32)


def on_device(amps, symmetry, screen, owner, integrals):
    n_pair = lax.axis_size("pair")
    local_rows, tile_count, tile_width = amps.shape
    per_owner = tile_count // n_pair
    owner_span = per_owner * tile_width
    tile_order = jnp.argsort(owner, stable=True).reshape(n_pair, per_owner)
    sorted_amps = jnp.take(amps, tile_order.reshape(-1), axis=1).reshape(
        local_rows, n_pair, owner_span
    )
    owned = lax.dynamic_index_in_dim(tile_order, lax.axis_index("pair"), 0, keepdims=False)
    labels = jnp.take(symmetry, owned)
    allowed = ((labels[:, None] == labels[None, :]) & (screen[0] == 1)).astype(jnp.bfloat16)
    mask_rows = jnp.repeat(allowed, tile_width, axis=0)
    block_rows = integrals[0]
    received = lax.all_to_all(sorted_amps, "pair", split_axis=1, concat_axis=1, tiled=True)
    flat_rows = received.reshape(local_rows * n_pair, owner_span)
    summed = contract(
        flat_rows,
        lax.all_gather(block_rows, "slab", axis=0, tiled=True),
        mask_rows,
        per_owner,
        tile_width,
    )
    product = summed.astype(jnp.bfloat16).reshape(local_rows, n_pair, owner_span)
    returned = lax.all_to_all(product, "pair", split_axis=1, concat_axis=1, tiled=True)
    return returned.reshape(local_rows, n_pair, per_owner, tile_width)


def solution(mesh):
    in_specs = (
        P(("pair", "slab"), None, None),
        P(),
        P("pair", None, None),
        P(),
        P("pair", "slab", None),
    )
    out_specs = P(("pair", "slab"), None, None, None)
    return jax.shard_map(
        on_device, mesh=mesh, in_specs=in_specs, out_specs=out_specs, check_vma=False
    )
```

profile of v0, /device:TPU:1, one launch (start us, length us, event | category | flops | bytes accessed | tf_op | source)
XLA Modules:
  0.0 163.3 jit_solution(9701086411608174818)
XLA Ops:
  6.5 0.7 all-gather.3.cloned.1.call-update
  7.3 5.1 %sort.17 = (s32[1024]{0:T(1024)}, s32[1024]{0:T(1024)S(1)}) sort(s32[1024]{0:T(1024)} %param.8, s32[1024]{0:T(1024)S(1)} %iota.4), dimensions={0}, to_apply=%region_0.0 | sort | flops 10240 | bytes 16384 | tf_op jit(solution)/shard_map/jit(argsort)/sort | solution.py:20
  12.3 0.1 broadcast_in_dim.25
  12.4 0.2 broadcast_in_dim.26
  12.6 0.1 copy.23
  12.7 0.0 copy-done
  12.7 4.4 %gather_fusion = bf16[1024,2,128]{2,0,1:T(8,128)(2,1)S(1)} fusion(bf16[2,1024,128]{2,1,0:T(8,128)(2,1)S(1)} %copy-done, s32[1024]{0:T(1024)S(1)} %fusion.5), kind=kCustom, calls=%fused_computation | custom fusion | bytes 1052672 | tf_op jit(solution)/shard_map/jit(_take)/gather | solution.py:21
  17.1 0.2 gather.13
  17.4 1.9 %broadcast_select_fusion = bf16[2,64,2048]{2,0,1:T(2,128)(2,1)} fusion(pred[64,2048]{1,0:T(8,128)(4,1)S(1)} %bitcast.43, bf16[2,64,2048]{2,1,0:T(8,128)(2,1)S(1)} %gather.13), kind=kLoop, calls=%fused_computation.7 | loop fusion | flops 262144 | bytes 1179648 | tf_op jit(solution)/shard_map/jit(_take)/select_n | solution.py:21
  19.2 14.8 %all-to-all-start = ((bf16[2,64,2048]{2,0,1:T(2,128)(2,1)}), bf16[2,64,2048]{2,0,1:T(2,128)(2,1)S(1)}, u32[]{:S(2)}, u32[]{:S(2)}) async-start(bf16[2,64,2048]{2,0,1:T(2,128)(2,1)} %broadcast_select_fusion), calls=%async_computation | async-start | bytes 1048576 | tf_op jit(solution)/shard_map/all_to_all | solution.py:29
  34.1 0.1 reshape.78
  34.2 0.6 gather_fusion.1
  34.9 0.0 copy-done.2
  34.9 0.1 fusion.4
  35.0 16.8 %all-to-all-done = bf16[2,64,2048]{2,0,1:T(2,128)(2,1)S(1)} async-done(((bf16[2,64,2048]{2,0,1:T(2,128)(2,1)}), bf16[2,64,2048]{2,0,1:T(2,128)(2,1)S(1)}, u32[]{:S(2)}, u32[]{:S(2)}) %all-to-all-start) | async-done | bytes 524320 | tf_op jit(solution)/shard_map/all_to_all | solution.py:29
  51.8 0.2 copy.10
  52.0 59.5 %all-gather.3.cloned.1.call-done = bf16[1,2048,2048]{2,1,0:T(8,128)(2,1)} async-done(((bf16[1,256,2048]{2,1,0:T(8,128)(2,1)}), bf16[1,2048,2048]{2,1,0:T(8,128)(2,1)}) %all-gather.3.cloned.1.call-update) | async-done | bytes 8388624 | tf_op jit(solution)/shard_map/all_gather | solution.py:33
  111.5 0.1 broadcast_in_dim.31
  111.5 9.0 %mul.14 = bf16[2048,16,128]{2,1,0:T(8,128)(2,1)S(1)} broadcast(bf16[2048,16]{1,0:T(8,128)(2,1)S(1)} %bitcast.41), dimensions={0,1} | broadcast | bytes 8454144 | tf_op jit(solution)/shard_map/mul | solution.py:10
  120.5 5.7 %fusion.3 = bf16[128,2048]{1,0:T(8,128)(2,1)S(1)} fusion(bf16[128,2048]{1,0:T(8,128)(2,1)S(1)} %bitcast.44, bf16[256,8,16,128]{3,2,1,0:T(8,128)(2,1)S(1)} %bitcast.40, bf16[1,2048,2048]{2,1,0:T(8,128)(2,1)S(1)} %copy-done.3), kind=kOutput, calls=%fused_computation.6 | convolution fusion | flops 1078198272 | bytes 17825792 | tf_op jit(solution)/shard_map/dot_general | solution.py:12
  126.2 0.5 copy.11
  126.7 28.5 %all_to_all.10 = bf16[2,64,2048]{2,0,1:T(2,128)(2,1)S(1)} all-to-all(bf16[2,64,2048]{2,0,1:T(2,128)(2,1)S(1)} %copy.11), channel_id=1, replica_groups=mesh['pair'=64,'slab'=8] {'pair'}, dimensions={1} | all-to-all | bytes 1048576 | tf_op jit(solution)/shard_map/all_to_all | solution.py:39
  155.3 0.3 reshape.80
  155.6 0.8 copy.12
  (14 shorter events, 0.1 us)
Async XLA Ops:
  6.5 6.2 %copy-start = (bf16[2,1024,128]{2,1,0:T(8,128)(2,1)S(1)}, bf16[2,1024,128]{2,1,0:T(8,128)(2,1)}, u32[]{:S(2)}) copy-start(bf16[2,1024,128]{2,1,0:T(8,128)(2,1)} %param.5) | copy-start | bytes 1572868
  6.5 27.7 %copy-start.1 = (s32[1024]{0:T(1024)S(1)}, s32[1024]{0:T(1024)}, u32[]{:S(2)}) copy-start(s32[1024]{0:T(1024)} %param.6) | copy-start | bytes 12292
  6.5 28.3 %copy-start.2 = (s32[1,16,16]{2,1,0:T(8,128)S(1)}, s32[1,16,16]{2,1,0:T(8,128)}, u32[]{:S(2)}) copy-start(s32[1,16,16]{2,1,0:T(8,128)} %param.7) | copy-start | bytes 3076
  6.5 104.9 %all-gather.3.cloned.1.call-start = ((), (), s32[]{:S(2)}) async-start(), calls=%async_computation.2 | async-start | bytes 9437184 | tf_op jit(solution)/shard_map/all_gather | solution.py:33
  19.2 32.6 %all-to-all-start = ((bf16[2,64,2048]{2,0,1:T(2,128)(2,1)}), bf16[2,64,2048]{2,0,1:T(2,128)(2,1)S(1)}, u32[]{:S(2)}, u32[]{:S(2)}) async-start(bf16[2,64,2048]{2,0,1:T(2,128)(2,1)} %broadcast_select_fusion), calls=%async_computation | async-start | bytes 1048576 | tf_op jit(solution)/shard_map/all_to_all | solution.py:29
  111.5 9.0 %copy-start.3 = (bf16[1,2048,2048]{2,1,0:T(8,128)(2,1)S(1)}, bf16[1,2048,2048]{2,1,0:T(8,128)(2,1)}, u32[]{:S(2)}) copy-start(bf16[1,2048,2048]{2,1,0:T(8,128)(2,1)} %all-gather.3.cloned.1.call-done) | copy-start | bytes 25165828
Sparse Core Ops, SparseCore 0:
  9.4 101.9 all-gather.2
where the time goes:
time: 164 us; the launch traced here: 163 us
  waiting for transfers between devices  77 us (47%)
  blocking collectives  28.5 us (17%)
  local copies, waits for them, and re-layouts  16.6 us (10%)
  starting transfers between devices  14.8 us (9%)
  between operations  13.6 us (8%)
  other arithmetic  7.06 us (4%)
  matrix products  5.67 us (3%)
    all_gather x1, waiting for transfers between devices, on_device(): lax.all_gather(block_rows, 'slab', axis=0, tiled=True)  59.5 us
    all_to_all x1, blocking collectives, on_device(): lax.all_to_all(product, 'pair', split_axis=1, concat_axis=1, tiled=True)  28.5 us
    all_to_all x1, waiting for transfers between devices, on_device(): lax.all_to_all(sorted_amps, 'pair', split_axis=1, concat_axis=1, tiled=True)  16.8 us
    all_to_all x1, starting transfers between devices, on_device(): lax.all_to_all(sorted_amps, 'pair', split_axis=1, concat_axis=1, tiled=True)  14.8 us
    mul x1, local copies, waits for them, and re-layouts, contract(): block_piece.reshape(rows_here, per_owner, tile_width)  8.96 us
    dot_general x1, matrix products, contract(): return jnp.dot(operand, masked, preferred_element_type=jnp.float32)  5.67 us
    sort x1, other arithmetic, on_device(): tile_order = jnp.argsort(owner, stable=True).reshape(n_pair, per_owner)  5.05 us
    gather x2, local copies, waits for them, and re-layouts, on_device(): jnp.take(amps, tile_order.reshape(-1), axis=1)  4.62 us
  transfers between devices with their start and end apart: 2, of which 2 were waited for; matrix products, arithmetic and copies ran while one was open for 8% of the time, Pallas kernels for 0%

commit v1 on v0

--- a/solution.py
+++ b/solution.py
@@ -2,6 +2,19 @@
 import jax.numpy as jnp
 from jax import lax
 from jax.sharding import PartitionSpec as P
+
+
+def collect(array, axis, dim):
+    ways = lax.axis_size(axis)
+    up = [(d, (d + 1) % ways) for d in range(ways)]
+    down = [(d, (d - 1) % ways) for d in range(ways)]
+    earlier, later = ([array], [array])
+    for _ in range(ways // 2):
+        earlier.append(lax.ppermute(earlier[-1], axis, up))
+    for _ in range((ways - 1) // 2):
+        later.append(lax.ppermute(later[-1], axis, down))
+    line = jnp.concatenate([*earlier[::-1], *later[1:]], axis=dim)
+    return jnp.roll(line, (lax.axis_index(axis) - ways // 2) * array.shape[dim], axis=dim)
 
 
 def contract(operand, block_piece, mask_piece, per_owner, tile_width):
@@ -28,13 +41,7 @@
     block_rows = integrals[0]
     received = lax.all_to_all(sorted_amps, "pair", split_axis=1, concat_axis=1, tiled=True)
     flat_rows = received.reshape(local_rows * n_pair, owner_span)
-    summed = contract(
-        flat_rows,
-        lax.all_gather(block_rows, "slab", axis=0, tiled=True),
-        mask_rows,
-        per_owner,
-        tile_width,
-    )
+    summed = contract(flat_rows, collect(block_rows, "slab", 0), mask_rows, per_owner, tile_width)
     product = summed.astype(jnp.bfloat16).reshape(local_rows, n_pair, owner_span)
     returned = lax.all_to_all(product, "pair", split_axis=1, concat_axis=1, tiled=True)
     return returned.reshape(local_rows, n_pair, per_owner, tile_width)

time: 164 us -> 196 us (1.20)
  starting transfers between devices: 14.8 us -> 48.6 us
  local copies, waits for them, and re-layouts: 16.6 us -> 36.3 us
  between operations: 13.6 us -> 0.32 us
  waiting for transfers between devices: 77 us -> 71.7 us
  blocking collectives: 28.5 us -> 23.7 us
    all_gather x1 -> x0, waiting for transfers between devices: 59.5 us -> none  [on_device(): lax.all_gather(block_rows, 'slab', axis=0, tiled=True)]
    ppermute x0 -> x7, waiting for transfers between devices: none -> 56.2 us  [the longest x4 40.4 us: collect(): earlier.append(lax.ppermute(earlier[-1], axis, up))]
    ppermute x0 -> x7, starting transfers between devices: none -> 28 us  [the longest x4 14.4 us: collect(): earlier.append(lax.ppermute(earlier[-1], axis, up))]
    unnamed x9 -> x20, local copies, waits for them, and re-layouts: 0.08 us -> 13.4 us
    all_to_all x1, starting transfers between devices: 14.8 us -> 20.6 us  [on_device(): lax.all_to_all(sorted_amps, 'pair', split_axis=1, concat_axis=1, tiled=True)]
    gather x2, local copies, waits for them, and re-layouts: 4.62 us -> 10.3 us  [on_device(): jnp.take(amps, tile_order.reshape(-1), axis=1)]
    all_to_all x1, blocking collectives: 28.5 us -> 23.7 us  [on_device(): lax.all_to_all(product, 'pair', split_axis=1, concat_axis=1, tiled=True)]
  transfers between devices with their start and end apart: 2 -> 8, of which waited for: 2 -> 5; matrix products, arithmetic and copies ran while one was open for 8% -> 14% of each run, Pallas kernels for 0% -> 0%
where the time goes in v1:
time: 196 us; the launch traced here: 194 us
  waiting for transfers between devices  71.7 us (37%)
  starting transfers between devices  48.6 us (25%)
  local copies, waits for them, and re-layouts  36.3 us (19%)
  blocking collectives  23.7 us (12%)
  other arithmetic  7.76 us (4%)
  matrix products  5.9 us (3%)
    ppermute x4, waiting for transfers between devices, collect(): earlier.append(lax.ppermute(earlier[-1], axis, up))  40.4 us
    all_to_all x1, blocking collectives, on_device(): lax.all_to_all(product, 'pair', split_axis=1, concat_axis=1, tiled=True)  23.7 us
    all_to_all x1, starting transfers between devices, on_device(): lax.all_to_all(sorted_amps, 'pair', split_axis=1, concat_axis=1, tiled=True)  20.6 us
    ppermute x3, waiting for transfers between devices, collect(): later.append(lax.ppermute(later[-1], axis, down))  15.8 us
    all_to_all x1, waiting for transfers between devices, on_device(): lax.all_to_all(sorted_amps, 'pair', split_axis=1, concat_axis=1, tiled=True)  15.5 us
    ppermute x4, starting transfers between devices, collect(): earlier.append(lax.ppermute(earlier[-1], axis, up))  14.4 us
    ppermute x3, starting transfers between devices, collect(): later.append(lax.ppermute(later[-1], axis, down))  13.6 us
    unnamed x20, local copies, waits for them, and re-layouts  13.4 us
  transfers between devices with their start and end apart: 8, of which 5 were waited for; matrix products, arithmetic and copies ran while one was open for 14% of the time, Pallas kernels for 0%

profile of v1, /device:TPU:1, one launch (start us, length us, event | category | flops | bytes accessed | tf_op | source)
XLA Modules:
  0.0 194.3 jit_solution(8331341670332986251)
XLA Ops:
  0.0 4.2 %collective-permute-start = (bf16[256,2048]{1,0:T(8,128)(2,1)}, bf16[256,2048]{1,0:T(8,128)(2,1)S(1)}, u32[]{:S(2)}, u32[]{:S(2)}) collective-permute-start(bf16[256,2048]{1,0:T(8,128)(2,1)} %bitcast.37), channel_id=1, source_target_pairs={{0,1},{1,2},{2,3},{3,4},{4,5},{5,6},{6,7},{7,0},{8,9},{9,10},{10,1... | collective-permute-start | bytes 3145736 | tf_op jit(solution)/shard_map/ppermute | solution.py:13
  4.2 19.8 %collective-permute-done = bf16[256,2048]{1,0:T(8,128)(2,1)S(1)} collective-permute-done((bf16[256,2048]{1,0:T(8,128)(2,1)}, bf16[256,2048]{1,0:T(8,128)(2,1)S(1)}, u32[]{:S(2)}, u32[]{:S(2)}) %collective-permute-start) | collective-permute-done | bytes 1048608 | tf_op jit(solution)/shard_map/ppermute | solution.py:13
  23.9 5.8 %collective-permute-start.1 = (bf16[256,2048]{1,0:T(8,128)(2,1)S(1)}, bf16[256,2048]{1,0:T(8,128)(2,1)}, u32[]{:S(2)}, u32[]{:S(2)}) collective-permute-start(bf16[256,2048]{1,0:T(8,128)(2,1)S(1)} %collective-permute-done), channel_id=1, source_target_pairs={{0,1},{1,2},{2,3},{3,4},{4,5},{5,6},{6,7},{7,0},{8,9},{9,10},{10,1... | collective-permute-start | bytes 3145736 | tf_op jit(solution)/shard_map/ppermute | solution.py:13
  29.8 4.3 %collective-permute-start.4 = (bf16[256,2048]{1,0:T(8,128)(2,1)}, bf16[256,2048]{1,0:T(8,128)(2,1)}, u32[]{:S(2)}, u32[]{:S(2)}) collective-permute-start(bf16[256,2048]{1,0:T(8,128)(2,1)} %bitcast.38), channel_id=1, source_target_pairs={{0,7},{1,0},{2,1},{3,2},{4,3},{5,4},{6,5},{7,6},{8,15},{9,8},{10,9... | collective-permute-start | bytes 3145736 | tf_op jit(solution)/shard_map/ppermute | solution.py:15
  34.1 18.6 %collective-permute-done.1 = bf16[256,2048]{1,0:T(8,128)(2,1)} collective-permute-done((bf16[256,2048]{1,0:T(8,128)(2,1)S(1)}, bf16[256,2048]{1,0:T(8,128)(2,1)}, u32[]{:S(2)}, u32[]{:S(2)}) %collective-permute-start.1) | collective-permute-done | bytes 1048608 | tf_op jit(solution)/shard_map/ppermute | solution.py:13
  52.7 2.1 %collective-permute-start.2 = (bf16[256,2048]{1,0:T(8,128)(2,1)}, bf16[256,2048]{1,0:T(8,128)(2,1)}, u32[]{:S(2)}, u32[]{:S(2)}) collective-permute-start(bf16[256,2048]{1,0:T(8,128)(2,1)} %collective-permute-done.1), channel_id=1, source_target_pairs={{0,1},{1,2},{2,3},{3,4},{4,5},{5,6},{6,7},{7,0},{8,9},{9,10},{10,1... | collective-permute-start | bytes 3145736 | tf_op jit(solution)/shard_map/ppermute | solution.py:13
  54.8 5.1 %sort.17 = (s32[1024]{0:T(1024)}, s32[1024]{0:T(1024)S(1)}) sort(s32[1024]{0:T(1024)} %param.8, s32[1024]{0:T(1024)S(1)} %iota.4), dimensions={0}, to_apply=%region_0.0 | sort | flops 10240 | bytes 16384 | tf_op jit(solution)/shard_map/jit(argsort)/sort | solution.py:33
  60.0 9.0 %gather_fusion = bf16[1024,2,128]{2,0,1:T(8,128)(2,1)} fusion(bf16[2,1024,128]{2,1,0:T(8,128)(2,1)S(1)} %copy-done, s32[1024]{0:T(1024)S(1)} %get-tuple-element.8), kind=kCustom, calls=%fused_computation | custom fusion | bytes 1052672 | tf_op jit(solution)/shard_map/jit(_take)/gather | solution.py:34
  70.6 4.4 %collective-permute-start.5 = (bf16[256,2048]{1,0:T(8,128)(2,1)}, bf16[256,2048]{1,0:T(8,128)(2,1)}, u32[]{:S(2)}, u32[]{:S(2)}) collective-permute-start(bf16[256,2048]{1,0:T(8,128)(2,1)} %collective-permute-done.4), channel_id=1, source_target_pairs={{0,7},{1,0},{2,1},{3,2},{4,3},{5,4},{6,5},{7,6},{8,15},{9,8},{10,9... | collective-permute-start | bytes 3145736 | tf_op jit(solution)/shard_map/ppermute | solution.py:15
  75.0 2.0 %collective-permute-done.2 = bf16[256,2048]{1,0:T(8,128)(2,1)} collective-permute-done((bf16[256,2048]{1,0:T(8,128)(2,1)}, bf16[256,2048]{1,0:T(8,128)(2,1)}, u32[]{:S(2)}, u32[]{:S(2)}) %collective-permute-start.2) | collective-permute-done | bytes 1048608 | tf_op jit(solution)/shard_map/ppermute | solution.py:13
  77.1 2.3 %collective-permute-start.3 = (bf16[256,2048]{1,0:T(8,128)(2,1)}, bf16[256,2048]{1,0:T(8,128)(2,1)}, u32[]{:S(2)}, u32[]{:S(2)}) collective-permute-start(bf16[256,2048]{1,0:T(8,128)(2,1)} %collective-permute-done.2), channel_id=1, source_target_pairs={{0,1},{1,2},{2,3},{3,4},{4,5},{5,6},{6,7},{7,0},{8,9},{9,10},{10,1... | collective-permute-start | bytes 3145736 | tf_op jit(solution)/shard_map/ppermute | solution.py:13
  79.4 1.9 broadcast_select_fusion
  81.3 20.6 %all-to-all-start = ((bf16[2,64,2048]{2,0,1:T(2,128)(2,1)}), bf16[2,64,2048]{2,0,1:T(2,128)(2,1)S(1)}, u32[]{:S(2)}, u32[]{:S(2)}) async-start(bf16[2,64,2048]{2,0,1:T(2,128)(2,1)} %broadcast_select_fusion), calls=%async_computation | async-start | bytes 1048576 | tf_op jit(solution)/shard_map/all_to_all | solution.py:42
  101.9 1.3 gather_fusion.1
  104.1 15.5 %all-to-all-done = bf16[2,64,2048]{2,0,1:T(2,128)(2,1)S(1)} async-done(((bf16[2,64,2048]{2,0,1:T(2,128)(2,1)}), bf16[2,64,2048]{2,0,1:T(2,128)(2,1)S(1)}, u32[]{:S(2)}, u32[]{:S(2)}) %all-to-all-start) | async-done | bytes 524320 | tf_op jit(solution)/shard_map/all_to_all | solution.py:42
  119.8 4.9 %collective-permute-start.6 = (bf16[256,2048]{1,0:T(8,128)(2,1)}, bf16[256,2048]{1,0:T(8,128)(2,1)S(1)}, u32[]{:S(2)}, u32[]{:S(2)}) collective-permute-start(bf16[256,2048]{1,0:T(8,128)(2,1)} %collective-permute-done.5), channel_id=1, source_target_pairs={{0,7},{1,0},{2,1},{3,2},{4,3},{5,4},{6,5},{7,6},{8,15},{9,8},{10,9... | collective-permute-start | bytes 3145736 | tf_op jit(solution)/shard_map/ppermute | solution.py:15
  125.9 1.3 constant_dynamic-update-slice_fusion.14
  128.7 1.3 constant_dynamic-update-slice_fusion.10
  131.3 15.8 %collective-permute-done.6 = bf16[256,2048]{1,0:T(8,128)(2,1)S(1)} collective-permute-done((bf16[256,2048]{1,0:T(8,128)(2,1)}, bf16[256,2048]{1,0:T(8,128)(2,1)S(1)}, u32[]{:S(2)}, u32[]{:S(2)}) %collective-permute-start.6) | collective-permute-done | bytes 1048608 | tf_op jit(solution)/shard_map/ppermute | solution.py:15
  147.2 1.3 constant_dynamic-update-slice_fusion.7
  148.5 1.3 constant_dynamic-update-slice_fusion.6
  154.0 9.0 %mul.18 = bf16[2048,16,128]{2,1,0:T(8,128)(2,1)S(1)} broadcast(bf16[2048,16]{1,0:T(8,128)(2,1)S(1)} %bitcast.39), dimensions={0,1} | broadcast | bytes 8454144 | tf_op jit(solution)/shard_map/mul | solution.py:23
  163.0 5.9 %fusion.3 = bf16[128,2048]{1,0:T(8,128)(2,1)S(1)} fusion(bf16[128,2048]{1,0:T(8,128)(2,1)S(1)} %bitcast.42, bf16[256,8,16,128]{3,2,1,0:T(8,128)(2,1)S(1)} %bitcast.36, bf16[4096,2048]{1,0:T(8,128)(2,1)S(1)} %constant_dynamic-update-slice_fusion, s32[]{:T(128)S(6)} %select_n.63), kind=kOutput, calls=%fused_computation.6 | convolution fusion | flops 1090781184 | bytes 17825796 | tf_op jit(solution)/shard_map/dot_general | solution.py:25
  169.4 23.7 %all_to_all.10 = bf16[2,64,2048]{2,0,1:T(2,128)(2,1)S(1)} all-to-all(bf16[2,64,2048]{2,0,1:T(2,128)(2,1)S(1)} %copy.11), channel_id=1, replica_groups=mesh['pair'=64,'slab'=8] {'pair'}, dimensions={1} | all-to-all | bytes 1048576 | tf_op jit(solution)/shard_map/all_to_all | solution.py:46
  (36 shorter events, 12.7 us)
Async XLA Ops:
  0.0 60.0 %copy-start = (bf16[2,1024,128]{2,1,0:T(8,128)(2,1)S(1)}, bf16[2,1024,128]{2,1,0:T(8,128)(2,1)}, u32[]{:S(2)}) copy-start(bf16[2,1024,128]{2,1,0:T(8,128)(2,1)} %param.5) | copy-start | bytes 1572868
  0.0 128.6 %copy-start.1 = (bf16[1,256,2048]{2,1,0:T(8,128)(2,1)S(1)}, bf16[1,256,2048]{2,1,0:T(8,128)(2,1)}, u32[]{:S(2)}) copy-start(bf16[1,256,2048]{2,1,0:T(8,128)(2,1)} %param.9) | copy-start | bytes 3145732
  0.0 23.9 %collective-permute-start = (bf16[256,2048]{1,0:T(8,128)(2,1)}, bf16[256,2048]{1,0:T(8,128)(2,1)S(1)}, u32[]{:S(2)}, u32[]{:S(2)}) collective-permute-start(bf16[256,2048]{1,0:T(8,128)(2,1)} %bitcast.37), channel_id=1, source_target_pairs={{0,1},{1,2},{2,3},{3,4},{4,5},{5,6},{6,7},{7,0},{8,9},{9,10},{10,1... | collective-permute-start | bytes 3145736 | tf_op jit(solution)/shard_map/ppermute | solution.py:13
  23.9 28.8 %collective-permute-start.1 = (bf16[256,2048]{1,0:T(8,128)(2,1)S(1)}, bf16[256,2048]{1,0:T(8,128)(2,1)}, u32[]{:S(2)}, u32[]{:S(2)}) collective-permute-start(bf16[256,2048]{1,0:T(8,128)(2,1)S(1)} %collective-permute-done), channel_id=1, source_target_pairs={{0,1},{1,2},{2,3},{3,4},{4,5},{5,6},{6,7},{7,0},{8,9},{9,10},{10,1... | collective-permute-start | bytes 3145736 | tf_op jit(solution)/shard_map/ppermute | solution.py:13
  29.8 40.8 %collective-permute-start.4 = (bf16[256,2048]{1,0:T(8,128)(2,1)}, bf16[256,2048]{1,0:T(8,128)(2,1)}, u32[]{:S(2)}, u32[]{:S(2)}) collective-permute-start(bf16[256,2048]{1,0:T(8,128)(2,1)} %bitcast.38), channel_id=1, source_target_pairs={{0,7},{1,0},{2,1},{3,2},{4,3},{5,4},{6,5},{7,6},{8,15},{9,8},{10,9... | collective-permute-start | bytes 3145736 | tf_op jit(solution)/shard_map/ppermute | solution.py:15
  52.7 24.4 %collective-permute-start.2 = (bf16[256,2048]{1,0:T(8,128)(2,1)}, bf16[256,2048]{1,0:T(8,128)(2,1)}, u32[]{:S(2)}, u32[]{:S(2)}) collective-permute-start(bf16[256,2048]{1,0:T(8,128)(2,1)} %collective-permute-done.1), channel_id=1, source_target_pairs={{0,1},{1,2},{2,3},{3,4},{4,5},{5,6},{6,7},{7,0},{8,9},{9,10},{10,1... | collective-permute-start | bytes 3145736 | tf_op jit(solution)/shard_map/ppermute | solution.py:13
  70.6 49.1 %collective-permute-start.5 = (bf16[256,2048]{1,0:T(8,128)(2,1)}, bf16[256,2048]{1,0:T(8,128)(2,1)}, u32[]{:S(2)}, u32[]{:S(2)}) collective-permute-start(bf16[256,2048]{1,0:T(8,128)(2,1)} %collective-permute-done.4), channel_id=1, source_target_pairs={{0,7},{1,0},{2,1},{3,2},{4,3},{5,4},{6,5},{7,6},{8,15},{9,8},{10,9... | collective-permute-start | bytes 3145736 | tf_op jit(solution)/shard_map/ppermute | solution.py:15
  77.1 47.5 %collective-permute-start.3 = (bf16[256,2048]{1,0:T(8,128)(2,1)}, bf16[256,2048]{1,0:T(8,128)(2,1)}, u32[]{:S(2)}, u32[]{:S(2)}) collective-permute-start(bf16[256,2048]{1,0:T(8,128)(2,1)} %collective-permute-done.2), channel_id=1, source_target_pairs={{0,1},{1,2},{2,3},{3,4},{4,5},{5,6},{6,7},{7,0},{8,9},{9,10},{10,1... | collective-permute-start | bytes 3145736 | tf_op jit(solution)/shard_map/ppermute | solution.py:13
  81.3 38.3 %all-to-all-start = ((bf16[2,64,2048]{2,0,1:T(2,128)(2,1)}), bf16[2,64,2048]{2,0,1:T(2,128)(2,1)S(1)}, u32[]{:S(2)}, u32[]{:S(2)}) async-start(bf16[2,64,2048]{2,0,1:T(2,128)(2,1)} %broadcast_select_fusion), calls=%async_computation | async-start | bytes 1048576 | tf_op jit(solution)/shard_map/all_to_all | solution.py:42
  119.8 27.3 %collective-permute-start.6 = (bf16[256,2048]{1,0:T(8,128)(2,1)}, bf16[256,2048]{1,0:T(8,128)(2,1)S(1)}, u32[]{:S(2)}, u32[]{:S(2)}) collective-permute-start(bf16[256,2048]{1,0:T(8,128)(2,1)} %collective-permute-done.5), channel_id=1, source_target_pairs={{0,7},{1,0},{2,1},{3,2},{4,3},{5,4},{6,5},{7,6},{8,15},{9,8},{10,9... | collective-permute-start | bytes 3145736 | tf_op jit(solution)/shard_map/ppermute | solution.py:15
